TPU v7x, 128 devices: a whole 4x4x4 slice. The times are simulated.
128 devices in a mesh: row: 8 (over z_lo, y), col: 16 (over z_hi, x, core).
Axes of the slice: x: 4, y: 4, z: 4 (z_hi: 2, z_lo: 2; z = z_hi * 2 + z_lo), core: 2. Of those that a mesh axis runs over, the one named last changes fastest.
Arguments:
- observed: float32 [4, 65536], P(None, ('row', 'col')), may hold values from -50 to 50
- tile_values: bfloat16 [256, 32, 256, 256], P('row', 'col'), may hold values from -2.2649514 to 2.2649514
- tile_cols: int32 [256, 32], P('row', 'col'), may hold values from 0 to 255
Outputs:
- solution: float32 [4, 1048576], P(None, ('col', 'row'))
- residual_ratio: float32 [4], replicated
All inputs are finite; a program needn't handle non-finite values.
Results may differ from a plain program's by a relative error of at most 0.0021.
Values may be sent and summed in bfloat16 or wider, within the bound.
A program may use at most 128 MiB of HBM per device.

v0:
```python
import jax
import jax.numpy as jnp
from jax import lax
from jax.sharding import PartitionSpec as P

ITERS = 2
N = 1048576
epsilon_sq = 1e-06


def local(observed, tile_values, tile_cols):
    right_sides = observed.shape[0]
    row_tiles = tile_values.shape[0]
    per_block = tile_values.shape[1]
    tile_size = tile_values.shape[2]
    col_tiles = N // (tile_size * lax.axis_size("col"))
    panel_len = col_tiles * tile_size
    share_len = panel_len // lax.axis_size("row")
    flat_cols = tile_cols.reshape(-1)

    def adjoint_map(left_bf):
        gathered = lax.all_gather(left_bf, "col", axis=1, tiled=True).reshape(
            right_sides, row_tiles, tile_size
        )
        tile_terms = jnp.einsum(
            "rktj,nrt->nrkj", tile_values, gathered, preferred_element_type=jnp.float32
        )
        tile_terms = tile_terms.reshape(right_sides, row_tiles * per_block, tile_size)
        placed = (
            jnp.zeros((right_sides, col_tiles, tile_size), jnp.float32)
            .at[:, flat_cols]
            .add(tile_terms)
        )
        placed = placed.reshape(right_sides, panel_len)
        summed = lax.psum_scatter(placed, "row", scatter_dimension=1, tiled=True)
        return summed

    def lanczos_pair(left_raw, right_vec):
        beta_sq = lax.psum(jnp.sum(left_raw * left_raw, axis=1), ("row", "col"))
        beta_norm = jnp.sqrt(beta_sq + epsilon_sq)
        product = adjoint_map(left_raw.astype(jnp.bfloat16))
        right_raw = product / beta_norm[:, None] - beta_norm[:, None] * right_vec
        alpha_sq = lax.psum(jnp.sum(right_raw * right_raw, axis=1), ("row", "col"))
        alpha_norm = jnp.sqrt(alpha_sq + epsilon_sq)
        return (beta_norm, alpha_norm, right_raw)

    blank_right = jnp.zeros((right_sides, share_len), jnp.float32)
    beta_norm, alpha_norm, right_raw = lanczos_pair(observed, blank_right)
    first_beta = beta_norm
    left_vec = observed / beta_norm[:, None]
    right_vec = right_raw / alpha_norm[:, None]
    right_bf = right_raw.astype(jnp.bfloat16)
    phibar = beta_norm
    rhobar = alpha_norm
    direction = right_vec
    solution = jnp.zeros_like(right_vec)
    for iteration in range(ITERS):
        whole_panel = lax.all_gather(right_bf, "row", axis=1, tiled=True)
        picked = jnp.take(whole_panel.reshape(right_sides, col_tiles, tile_size), tile_cols, axis=1)
        partial_rows = jnp.einsum(
            "rktj,nrkj->nrt", tile_values, picked, preferred_element_type=jnp.float32
        )
        left_raw = (
            lax.psum_scatter(
                partial_rows.reshape(right_sides, row_tiles * tile_size),
                "col",
                scatter_dimension=1,
                tiled=True,
            )
            / alpha_norm[:, None]
            - alpha_norm[:, None] * left_vec
        )
        beta_norm, alpha_norm, right_raw = lanczos_pair(left_raw, right_vec)
        left_vec = left_raw / beta_norm[:, None]
        right_vec = right_raw / alpha_norm[:, None]
        right_bf = right_raw.astype(jnp.bfloat16)
        rho_val = jnp.sqrt(rhobar * rhobar + beta_norm * beta_norm)
        cosine = rhobar / rho_val
        sine_val = beta_norm / rho_val
        theta_val = sine_val * alpha_norm
        rhobar = -cosine * alpha_norm
        phi_val = cosine * phibar
        phibar = sine_val * phibar
        solution = solution + (phi_val / rho_val)[:, None] * direction
        direction = right_vec - (theta_val / rho_val)[:, None] * direction
    return (solution, phibar / first_beta)


def solution(mesh):
    in_specs = (P(None, ("row", "col")), P("row", "col", None, None), P("row", "col"))
    out_specs = (P(None, ("col", "row")), P())
    return jax.shard_map(local, mesh=mesh, in_specs=in_specs, out_specs=out_specs, check_vma=False)
```

profile of v0, /device:TPU:1, one launch (start us, length us, event | category | flops | bytes accessed | tf_op | source)
XLA Modules:
  0.0 1160.2 jit_solution(9524676217768432283)
XLA Ops:
  8.1 26.5 %all_gather.12 = bf16[4,8192]{1,0:T(4,128)(2,1)S(1)} all-gather(bf16[4,512]{1,0:T(4,128)(2,1)S(1)} %get-tuple-element.13), channel_id=1, replica_groups=mesh['row'=8,'col'=16] {'col'}, dimensions={1}, use_global_device_ids=true | all-gather | bytes 69632 | tf_op jit(solution)/shard_map/all_gather | solution.py:22
  35.5 4.6 fusion.21
  40.2 2.8 scatter_fusion
  43.0 16.1 %copy.26 = f32[4,65536]{0,1:T(8,128)} copy(f32[4,65536]{1,0:T(4,128)S(1)} %bitcast.65) | data formatting | bytes 2097152
  59.2 369.9 %psum.35 = f32[4]{0:T(128)S(1)} all-reduce(f32[4]{0:T(128)S(1)} %get-tuple-element.14), channel_id=1, replica_groups=mesh['row'=8,'col'=16] {'row','col'}, use_global_device_ids=true, to_apply=%region_3.0 | all-reduce | flops 4 | bytes 32 | tf_op jit(solution)/shard_map/psum | solution.py:39
  429.5 2.8 copy.27
  432.6 22.8 %all_gather.13 = bf16[4,65536]{1,0:T(4,128)(2,1)S(1)} all-gather(bf16[4,8192]{1,0:T(4,128)(2,1)S(1)} %convert_element_type.13), channel_id=1, replica_groups=mesh['row'=8,'col'=16] {'row'}, dimensions={1}, use_global_device_ids=true | all-gather | bytes 589824 | tf_op jit(solution)/shard_map/all_gather | solution.py:58
  456.1 5.7 fusion.2
  461.8 2.6 copy.28
  464.5 74.8 %psum.36 = f32[4]{0:T(128)S(1)} all-reduce(f32[4]{0:T(128)S(1)} %get-tuple-element.11), channel_id=1, replica_groups=mesh['row'=8,'col'=16] {'row','col'}, use_global_device_ids=true, to_apply=%region_5.0 | all-reduce | flops 4 | bytes 32 | tf_op jit(solution)/shard_map/psum | solution.py:43
  539.4 8.0 reduce-scatter.15.cloned.1.call-done
  547.4 1.1 copy.29
  548.7 23.2 %all_gather.14 = bf16[4,8192]{1,0:T(4,128)(2,1)S(1)} all-gather(bf16[4,512]{1,0:T(4,128)(2,1)S(1)} %convert_element_type.14), channel_id=1, replica_groups=mesh['row'=8,'col'=16] {'col'}, dimensions={1}, use_global_device_ids=true | all-gather | bytes 69632 | tf_op jit(solution)/shard_map/all_gather | solution.py:22
  571.8 4.6 fusion.22
  576.6 2.8 scatter_fusion.1
  579.4 16.1 %copy.30 = f32[4,65536]{0,1:T(8,128)} copy(f32[4,65536]{1,0:T(4,128)S(1)} %bitcast.64) | data formatting | bytes 2097152
  595.6 371.7 %psum.37 = f32[4]{0:T(128)S(1)} all-reduce(f32[4]{0:T(128)S(1)} %get-tuple-element.9), channel_id=1, replica_groups=mesh['row'=8,'col'=16] {'row','col'}, use_global_device_ids=true, to_apply=%region_8.10 | all-reduce | flops 4 | bytes 32 | tf_op jit(solution)/shard_map/psum | solution.py:39
  967.3 2.8 copy.31
  970.3 23.0 %all_gather.15 = bf16[4,65536]{1,0:T(4,128)(2,1)S(1)} all-gather(bf16[4,8192]{1,0:T(4,128)(2,1)S(1)} %get-tuple-element.7), channel_id=1, replica_groups=mesh['row'=8,'col'=16] {'row'}, dimensions={1}, use_global_device_ids=true | all-gather | bytes 589824 | tf_op jit(solution)/shard_map/all_gather | solution.py:58
  994.0 5.7 fusion
  999.7 2.6 copy.32
  1002.5 75.0 %psum.38 = f32[4]{0:T(128)S(1)} all-reduce(f32[4]{0:T(128)S(1)} %multiply_reduce_fusion), channel_id=1, replica_groups=mesh['row'=8,'col'=16] {'row','col'}, use_global_device_ids=true, to_apply=%region_12.14 | all-reduce | flops 4 | bytes 32 | tf_op jit(solution)/shard_map/psum | solution.py:43
  1077.5 8.0 reduce-scatter.19.cloned.1.call-done
  1086.7 65.6 %psum.39 = f32[4]{0:T(128)S(1)} all-reduce(f32[4]{0:T(128)S(1)} %fusion.11), channel_id=1, replica_groups=mesh['row'=8,'col'=16] {'row','col'}, use_global_device_ids=true, to_apply=%region_15.17 | all-reduce | flops 4 | bytes 32 | tf_op jit(solution)/shard_map/psum | solution.py:39
  (43 shorter events, 7.5 us)
Async XLA Ops:
  7.2 422.3 %reduce-scatter.13.cloned.1.call-start = ((), (), s32[]{:S(2)}) async-start(), calls=%async_computation.4 | async-start | bytes 37748736
  59.1 370.0 %copy-start.1 = (s32[32,2]{0,1:T(2,128)S(1)}, s32[32,2]{0,1:T(2,128)}, u32[]{:S(2)}) copy-start(s32[32,2]{0,1:T(2,128)} %param.7) | copy-start | bytes 772
  59.1 488.2 %reduce-scatter.15.cloned.1.call-start = ((), (), s32[]{:S(2)}) async-start(), calls=%async_computation.5 | async-start | bytes 4456448
  456.1 92.3 %copy-start = (f32[4,512]{1,0:T(4,128)S(1)}, f32[4,512]{1,0:T(4,128)}, u32[]{:S(2)}) copy-start(f32[4,512]{1,0:T(4,128)} %param.5) | copy-start | bytes 24580
  464.5 502.9 %reduce-scatter.17.cloned.1.call-start = ((), (), s32[]{:S(2)}) async-start(), calls=%async_computation.6 | async-start | bytes 37748736
  595.5 490.0 %reduce-scatter.19.cloned.1.call-start = ((), (), s32[]{:S(2)}) async-start(), calls=%async_computation.7 | async-start | bytes 4456448
Sparse Core Ops, SparseCore 0:
  59.3 325.6 reduce-scatter.12
  464.6 82.7 reduce-scatter.14
  595.6 327.5 reduce-scatter.16
  1002.6 82.7 reduce-scatter.18
where the time goes:
time: 1160 us
  blocking collectives  1050 us (91%)
  local copies, waits for them, and re-layouts  48 us (4%)
  matrix products  20.5 us (2%)
  waiting for transfers between devices  16.1 us (1%)
  between operations  13.9 us (1%)
    psum x3, blocking collectives, lanczos_pair(): beta_sq = lax.psum(jnp.sum(left_raw * left_raw, axis=1), ('row', 'col'))  807 us
    psum x2, blocking collectives, lanczos_pair(): alpha_sq = lax.psum(jnp.sum(right_raw * right_raw, axis=1), ('row', 'col'))  150 us
    all_gather x2, blocking collectives, adjoint_map(): lax.all_gather(left_bf, 'col', axis=1, tiled=True)  49.7 us
    unnamed x13, local copies, waits for them, and re-layouts  46 us
    all_gather x2, blocking collectives, local(): whole_panel = lax.all_gather(right_bf, 'row', axis=1, tiled=True)  45.8 us
  transfers between devices with their start and end apart: 4, of which 2 were waited for; matrix products, arithmetic and copies ran while one was open for 0% of the time, Pallas kernels for 0%

commit v1 on v0

--- a/solution.py
+++ b/solution.py
@@ -36,7 +36,9 @@
         return summed
 
     def lanczos_pair(left_raw, right_vec):
-        beta_sq = lax.psum(jnp.sum(left_raw * left_raw, axis=1), ("row", "col"))
+        beta_sq = jnp.sum(
+            lax.all_gather(jnp.sum(left_raw * left_raw, axis=1), ("row", "col")), axis=0
+        )
         beta_norm = jnp.sqrt(beta_sq + epsilon_sq)
         product = adjoint_map(left_raw.astype(jnp.bfloat16))
         right_raw = product / beta_norm[:, None] - beta_norm[:, None] * right_vec

time: 1160 us -> 1230 us (1.060)
  waiting for transfers between devices: 16.1 us -> 90.6 us
    unnamed x0 -> x3, blocking collectives: none -> 809 us
    psum x3 -> x0, blocking collectives: 807 us -> none  [lanczos_pair(): beta_sq = lax.psum(jnp.sum(left_raw * left_raw, axis=1), ('row', 'col'))]
    unnamed x8, waiting for transfers between devices: 16.1 us -> 90.6 us
    psum x2, blocking collectives: 150 us -> 138 us  [lanczos_pair(): alpha_sq = lax.psum(jnp.sum(right_raw * right_raw, axis=1), ('row', 'col'))]
    unnamed x13 -> x19, local copies, waits for them, and re-layouts: 46 us -> 46.7 us
where the time goes in v1:
time: 1230 us
  blocking collectives  1040 us (85%)
  waiting for transfers between devices  90.6 us (7%)
  local copies, waits for them, and re-layouts  49.1 us (4%)
  matrix products  20.5 us (2%)
  between operations  14 us (1%)
    unnamed x3, blocking collectives  809 us
    psum x2, blocking collectives, lanczos_pair(): alpha_sq = lax.psum(jnp.sum(right_raw * right_raw, axis=1), ('row', 'col'))  138 us
    unnamed x8, waiting for transfers between devices  90.6 us
    all_gather x2, blocking collectives, adjoint_map(): lax.all_gather(left_bf, 'col', axis=1, tiled=True)  49.6 us
    unnamed x19, local copies, waits for them, and re-layouts  46.7 us
    all_gather x2, blocking collectives, local(): whole_panel = lax.all_gather(right_bf, 'row', axis=1, tiled=True)  45.7 us
  transfers between devices with their start and end apart: 4, of which 2 were waited for; matrix products, arithmetic and copies ran while one was open for 0% of the time, Pallas kernels for 0%

profile of v1, /device:TPU:1, one launch (start us, length us, event | category | flops | bytes accessed | tf_op | source)
XLA Modules:
  0.0 1225.1 jit_solution(4320062039801442796)
XLA Ops:
  9.0 26.5 %all_gather.30 = bf16[4,8192]{1,0:T(4,128)(2,1)S(1)} all-gather(bf16[4,512]{1,0:T(4,128)(2,1)S(1)} %get-tuple-element.13), channel_id=1, replica_groups=mesh['row'=8,'col'=16] {'col'}, dimensions={1}, use_global_device_ids=true | all-gather | bytes 69632 | tf_op jit(solution)/shard_map/all_gather | solution.py:22
  35.5 4.6 fusion.21
  40.2 2.8 scatter_fusion
  43.1 16.1 %copy.26 = f32[4,65536]{0,1:T(8,128)} copy(f32[4,65536]{1,0:T(4,128)S(1)} %bitcast.65) | data formatting | bytes 2097152
  59.5 371.6 %all-reduce = f32[512]{0:T(512)S(1)} all-reduce(f32[512]{0:T(512)S(1)} %dynamic-update-slice), channel_id=2, replica_groups=mesh['row'=8,'col'=16] {'row','col'}, use_global_device_ids=true, to_apply=%add | all-reduce | flops 512 | bytes 4096
  431.6 2.8 copy.27
  434.7 62.5 %psum.14 = f32[4]{0:T(128)S(1)} all-reduce(f32[4]{0:T(128)S(1)} %get-tuple-element.11), channel_id=1, replica_groups=mesh['row'=8,'col'=16] {'row','col'}, use_global_device_ids=true, to_apply=%region_5.0 | all-reduce | flops 4 | bytes 32 | tf_op jit(solution)/shard_map/psum | solution.py:45
  497.3 22.9 %all_gather.33 = bf16[4,65536]{1,0:T(4,128)(2,1)S(1)} all-gather(bf16[4,8192]{1,0:T(4,128)(2,1)S(1)} %convert_element_type.13), channel_id=1, replica_groups=mesh['row'=8,'col'=16] {'row'}, dimensions={1}, use_global_device_ids=true | all-gather | bytes 589824 | tf_op jit(solution)/shard_map/all_gather | solution.py:60
  520.9 5.7 fusion.2
  526.5 2.6 copy.28
  529.2 82.5 %reduce-scatter.15.cloned.1.call-done = f32[512,4]{1,0:T(8,128)} async-done(((f32[8192,4]{1,0:T(8,128)}), f32[512,4]{1,0:T(8,128)}) %reduce-scatter.15.cloned.1.call-update) | async-done | bytes 8208
  611.8 1.1 copy.29
  613.0 23.1 %all_gather.36 = bf16[4,8192]{1,0:T(4,128)(2,1)S(1)} all-gather(bf16[4,512]{1,0:T(4,128)(2,1)S(1)} %convert_element_type.14), channel_id=1, replica_groups=mesh['row'=8,'col'=16] {'col'}, dimensions={1}, use_global_device_ids=true | all-gather | bytes 69632 | tf_op jit(solution)/shard_map/all_gather | solution.py:22
  636.2 4.6 fusion.22
  640.9 2.8 scatter_fusion.1
  643.7 16.1 %copy.30 = f32[4,65536]{0,1:T(8,128)} copy(f32[4,65536]{1,0:T(4,128)S(1)} %bitcast.64) | data formatting | bytes 2097152
  660.1 371.8 %all-reduce.1 = f32[512]{0:T(512)S(1)} all-reduce(f32[512]{0:T(512)S(1)} %dynamic-update-slice.1), channel_id=3, replica_groups=mesh['row'=8,'col'=16] {'row','col'}, use_global_device_ids=true, to_apply=%add.1 | all-reduce | flops 512 | bytes 4096
  1032.1 2.8 copy.31
  1035.1 22.8 %all_gather.37 = bf16[4,65536]{1,0:T(4,128)(2,1)S(1)} all-gather(bf16[4,8192]{1,0:T(4,128)(2,1)S(1)} %get-tuple-element.7), channel_id=1, replica_groups=mesh['row'=8,'col'=16] {'row'}, dimensions={1}, use_global_device_ids=true | all-gather | bytes 589824 | tf_op jit(solution)/shard_map/all_gather | solution.py:60
  1058.6 5.7 fusion
  1064.3 2.6 copy.32
  1067.1 75.0 %psum.15 = f32[4]{0:T(128)S(1)} all-reduce(f32[4]{0:T(128)S(1)} %multiply_reduce_fusion), channel_id=1, replica_groups=mesh['row'=8,'col'=16] {'row','col'}, use_global_device_ids=true, to_apply=%region_12.14 | all-reduce | flops 4 | bytes 32 | tf_op jit(solution)/shard_map/psum | solution.py:45
  1142.1 7.9 reduce-scatter.19.cloned.1.call-done
  1151.5 65.5 %all-reduce.2 = f32[512]{0:T(512)S(1)} all-reduce(f32[512]{0:T(512)S(1)} %dynamic-update-slice.2), channel_id=4, replica_groups=mesh['row'=8,'col'=16] {'row','col'}, use_global_device_ids=true, to_apply=%add.2 | all-reduce | flops 512 | bytes 4096
  (55 shorter events, 8.6 us)
Async XLA Ops:
  7.2 424.4 %reduce-scatter.13.cloned.1.call-start = ((), (), s32[]{:S(2)}) async-start(), calls=%async_computation.4 | async-start | bytes 37748736
  59.1 372.1 %copy-start.1 = (s32[32,2]{0,1:T(2,128)S(1)}, s32[32,2]{0,1:T(2,128)}, u32[]{:S(2)}) copy-start(s32[32,2]{0,1:T(2,128)} %param.7) | copy-start | bytes 772
  59.2 552.6 %reduce-scatter.15.cloned.1.call-start = ((), (), s32[]{:S(2)}) async-start(), calls=%async_computation.5 | async-start | bytes 4456448
  520.9 92.0 %copy-start = (f32[4,512]{1,0:T(4,128)S(1)}, f32[4,512]{1,0:T(4,128)}, u32[]{:S(2)}) copy-start(f32[4,512]{1,0:T(4,128)} %param.5) | copy-start | bytes 24580
  529.2 502.9 %reduce-scatter.17.cloned.1.call-start = ((), (), s32[]{:S(2)}) async-start(), calls=%async_computation.6 | async-start | bytes 37748736
  659.8 490.2 %reduce-scatter.19.cloned.1.call-start = ((), (), s32[]{:S(2)}) async-start(), calls=%async_computation.7 | async-start | bytes 4456448
Sparse Core Ops, SparseCore 0:
  59.3 325.7 reduce-scatter.12
  529.3 82.4 reduce-scatter.14
  660.0 327.8 reduce-scatter.16
  1067.2 82.7 reduce-scatter.18
